TPU v7x, 32 devices: a whole 2x2x4 slice. The times are simulated.
32 devices in a mesh: passage: 2 (over x), brick: 16 (over z, y, core).
Axes of the slice: x: 2, y: 2, z: 4, core: 2. Of those that a mesh axis runs over, the one named last changes fastest.
Arguments:
- jac_blocks: bfloat16 [2, 25, 16, 8192], P('passage', None, None, 'brick'), may hold values from -6 to 6
- psi_start: float32 [2, 10, 16, 64, 128], P('passage', None, 'brick'), may hold values from -6 to 6
- source: float32 [2, 10, 16, 64, 128], P('passage', None, 'brick'), may hold values from -6 to 6
- pseudo_step: float32 [2, 16, 64, 128], P('passage', 'brick'), may hold values from 0.1 to 0.4
- dissipation: float32 [2, 16, 64, 128], P('passage', 'brick'), may hold values from 0.04 to 0.15
- freq_volume: float32 [2, 16, 64, 128], P('passage', 'brick'), may hold values from 0.2 to 2
- normals: float32 [2, 3, 16, 64], P('passage', None, 'brick'), may hold values from -6 to 6
- face_owner: int32 [2, 1024, 1], P('passage', 'brick'), may hold values from 0 to 15; in each aligned block of 64 rows (0 to 63, 64 to 127, ..., all dimensions but the last counted through in order) at most 16 rows name the same one
- face_slot: int32 [2, 1024], P('passage', 'brick'), may hold values from 0 to 255
Outputs:
- adjoint: float32 [2, 10, 16, 64, 128], P('passage', None, 'brick')
- sensitivity: float32 [2, 6, 4096], P('passage', None, 'brick')
Inputs may be any that keep to these rules, and one draw needn't show every extreme that they name: `face_owner`: in the 64 faces of one device (aligned blocks of the rows), no brick is named by more than 16 faces, and in some block some brick is named by exactly 16.
All inputs are finite; a program needn't handle non-finite values.
Results may differ from a plain program's by a relative error of at most 0.0003.
Values may be sent and summed in bfloat16 or wider, within the bound.
A program may use at most 64 MiB of HBM per device.

v0:
```python
import math
import jax
import jax.numpy as jnp
from jax import lax
from jax.sharding import PartitionSpec as P

NODE_DEV = 256
SWEEPS = 2
ND = 1
BLADES = 36


def padded(value, sides, width, wrap):
    for axis, dim in sides:
        peers, length = (lax.axis_size(axis), value.shape[dim])
        up = [(i, (i + 1) % peers) for i in range(peers if wrap else peers - 1)]
        down = [(j, i) for i, j in up]
        last = lax.slice_in_dim(value, length - width, length, axis=dim)
        initial = lax.slice_in_dim(value, 0, width, axis=dim)
        before = lax.ppermute(last, axis, up)
        after = lax.ppermute(initial, axis, down)
        value = jnp.concatenate([before, value, after], axis=dim)
    return value


def rotate(rim, turn):
    cosine = math.cos(turn)
    sine = math.sin(turn)
    real_part = rim[:, :5]
    imag_part = rim[:, 5:]
    return jnp.concatenate(
        [real_part * cosine - imag_part * sine, real_part * sine + imag_part * cosine], axis=1
    )


def transpose_apply(tiles, diff):
    total_real = jnp.zeros_like(diff[:, :5])
    total_imag = jnp.zeros_like(diff[:, :5])
    for row_index in range(5):
        column = tiles[:, row_index * 5 : row_index * 5 + 5].astype(jnp.float32)
        total_real = total_real + column * diff[:, row_index : row_index + 1]
        total_imag = total_imag + column * diff[:, 5 + row_index : 6 + row_index]
    return jnp.concatenate([total_real, total_imag], axis=1)


def advance(
    state,
    source,
    pseudo_step,
    dissipation,
    freq_volume,
    convect_fn,
    cycle_index,
    passes,
    phase_angle,
):
    padded_i = padded(state, (("brick", 2),), 1, False)
    padded_j = padded(state.astype(jnp.bfloat16), (("passage", 3),), 1, True).astype(state.dtype)
    below_rim = padded_j[:, :, :, :1]
    above_rim = padded_j[:, :, :, -1:]
    below_rim = jnp.where(cycle_index == 0, rotate(below_rim, -phase_angle), below_rim)
    above_rim = jnp.where(cycle_index == passes - 1, rotate(above_rim, phase_angle), above_rim)
    fixed_j = jnp.concatenate([below_rim, state, above_rim], axis=3)
    padded_k = jnp.pad(state, ((0, 0), (0, 0), (0, 0), (0, 0), (1, 1)))
    beside = padded_i[:, :, 2:] + padded_i[:, :, :-2]
    beside = beside + fixed_j[:, :, :, 2:] + fixed_j[:, :, :, :-2]
    beside = beside + padded_k[..., 2:] + padded_k[..., :-2]
    diff = 0.5 * (padded_i[:, :, 2:] - padded_i[:, :, :-2])
    convect = convect_fn(diff)
    omega = freq_volume[:, None]
    spin = jnp.concatenate([omega * state[:, 5:], -omega * state[:, :5]], axis=1)
    resid = convect + spin + dissipation[:, None] * (6.0 * state - beside) - source
    return state - pseudo_step[:, None] * resid


def body(
    jac_blocks,
    psi_start,
    source,
    pseudo_step,
    dissipation,
    freq_volume,
    normals,
    face_owner,
    face_slot,
):
    passes = lax.axis_size("passage")
    cycle_index = lax.axis_index("passage")
    bricks = lax.axis_size("brick")
    planes = psi_start.shape[2]
    width_j = psi_start.shape[3]
    width_k = psi_start.shape[4]
    phase_angle = 2.0 * math.pi * ND * passes / BLADES
    relaid = lax.all_to_all(jac_blocks, "brick", split_axis=2, concat_axis=3, tiled=True)
    tiles = relaid.reshape(1, 25, planes, width_j, width_k)

    def convect_fn(diff):
        return transpose_apply(tiles, diff)

    state = psi_start
    for sweep in range(SWEEPS):
        state = advance(
            state,
            source,
            pseudo_step,
            dissipation,
            freq_volume,
            convect_fn,
            cycle_index,
            passes,
            phase_angle,
        )
    wall_state = state[0, :, :, :, 0]
    face_normals = normals[0]
    values = jnp.concatenate(
        [face_normals * wall_state[1:4], face_normals * wall_state[6:9]], axis=0
    )
    values = values.reshape(6, planes * width_j)
    owners = face_owner[0, :, 0]
    slots = face_slot[0]
    node_ids = owners * NODE_DEV + slots
    local_terms = jnp.zeros((6, NODE_DEV * bricks), jnp.float32).at[:, node_ids].add(values)
    summed = lax.psum_scatter(local_terms, "brick", scatter_dimension=1, tiled=True)
    sensitivity = summed[None]
    return (state, sensitivity)


def solution(mesh):
    placed = (
        P("passage", None, None, "brick"),
        P("passage", None, "brick", None, None),
        P("passage", None, "brick", None, None),
        P("passage", "brick", None, None),
        P("passage", "brick", None, None),
        P("passage", "brick", None, None),
        P("passage", None, "brick", None),
        P("passage", "brick", None),
        P("passage", "brick"),
    )
    return jax.shard_map(
        body,
        mesh=mesh,
        in_specs=placed,
        out_specs=(P("passage", None, "brick", None, None), P("passage", None, "brick")),
        check_vma=False,
    )
```

profile of v0, /device:TPU:0, one launch (start us, length us, event | category | flops | bytes accessed | tf_op | source)
XLA Modules:
  0.0 128.0 jit_solution(5724360956886795302)
XLA Ops:
  7.2 0.0 copy-start
  7.2 0.0 copy-start.3
  7.2 0.0 copy-start.7
  7.2 0.0 copy-start.8
  7.2 2.5 %collective-permute-start.1 = (f32[1,10,1,64,128]{4,3,1,2,0:T(8,128)}, f32[1,10,1,64,128]{4,3,1,2,0:T(8,128)S(1)}, u32[]{:S(2)}, u32[]{:S(2)}) collective-permute-start(f32[1,10,1,64,128]{4,3,1,2,0:T(8,128)} %bitcast.71), channel_id=1, source_target_pairs={{0,1},{1,2},{2,3},{3,4},{4,5},{5,6},{6,7},{7,8},{8,9},{9,10},{10,1... | collective-permute-start | bytes 983048 | tf_op jit(solution)/shard_map/ppermute | solution.py:20
  9.8 1.3 %collective-permute-start = (f32[1,10,1,64,128]{4,3,1,2,0:T(8,128)}, f32[1,10,1,64,128]{4,3,1,2,0:T(8,128)S(1)}, u32[]{:S(2)}, u32[]{:S(2)}) collective-permute-start(f32[1,10,1,64,128]{4,3,1,2,0:T(8,128)} %bitcast.72), channel_id=1, source_target_pairs={{1,0},{2,1},{3,2},{4,3},{5,4},{6,5},{7,6},{8,7},{9,8},{10,9},{11,1... | collective-permute-start | bytes 983048 | tf_op jit(solution)/shard_map/ppermute | solution.py:21
  11.1 1.0 bitcast_convert_fusion
  12.1 2.4 %collective-permute-start.2 = (bf16[1,10,1,1,128]{4,3,1,2,0:T(2,128)(2,1)S(1)}, bf16[1,10,1,1,128]{4,3,1,2,0:T(2,128)(2,1)S(1)}, u32[]{:S(2)}, u32[]{:S(2)}) collective-permute-start(bf16[1,10,1,1,128]{4,3,1,2,0:T(2,128)(2,1)S(1)} %get-tuple-element.64), channel_id=1, source_target_pairs={{0,16},{16,0},{1,17},{17,1},{2,18},{18,2},{3,19},{19,3},{4,20},{20... | collective-permute-start | bytes 7688 | tf_op jit(solution)/shard_map/ppermute | solution.py:20
  14.5 0.1 collective-permute-start.3
  14.5 2.0 %copy.66 = bf16[1,25,16,512]{3,1,0,2:T(8,128)(2,1)} copy(bf16[1,25,16,512]{3,2,1,0:T(8,128)(2,1)} %param.9) | data formatting | bytes 819200 | tf_op args[0]
  16.6 8.9 %all-to-all-start = ((bf16[1,25,16,512]{3,1,0,2:T(8,128)(2,1)}), bf16[1,25,16,512]{3,1,0,2:T(8,128)(2,1)S(1)}, u32[]{:S(2)}, u32[]{:S(2)}) async-start(bf16[1,25,16,512]{3,1,0,2:T(8,128)(2,1)} %copy.66), calls=%async_computation | async-start | bytes 1048576 | tf_op jit(solution)/shard_map/all_to_all | solution.py:94
  25.5 0.0 reduce-scatter.2.cloned.1.call-start
  25.6 0.0 copy-done.3
  25.6 0.0 copy-done
  25.6 0.0 copy-done.7
  25.6 0.0 copy-done.8
  25.7 0.0 collective-permute-done.2
  25.7 0.0 collective-permute-done.3
  25.8 0.0 collective-permute-done.1
  25.8 0.0 collective-permute-done
  25.8 0.0 copy-start.1
  25.8 0.0 copy-start.4
  25.9 0.0 copy-start.5
  25.9 13.9 %all-to-all-done = bf16[1,25,16,512]{3,1,0,2:T(8,128)(2,1)S(1)} async-done(((bf16[1,25,16,512]{3,1,0,2:T(8,128)(2,1)}), bf16[1,25,16,512]{3,1,0,2:T(8,128)(2,1)S(1)}, u32[]{:S(2)}, u32[]{:S(2)}) %all-to-all-start) | async-done | bytes 409632 | tf_op jit(solution)/shard_map/all_to_all | solution.py:94
  39.8 0.2 copy.67
  40.0 0.2 reshape.329
  40.3 0.1 fusion.29
  40.4 0.1 fusion.25
  40.5 0.0 copy-done.1
  40.5 0.0 copy-done.4
  40.5 0.0 copy-done.5
  40.5 0.3 fusion.50
  40.8 1.6 %collective-permute-start.6 = (bf16[1,10,1,1,128]{4,3,1,2,0:T(2,128)(2,1)S(1)}, bf16[1,10,1,1,128]{4,3,1,2,0:T(2,128)(2,1)S(1)}, u32[]{:S(2)}, u32[]{:S(2)}) collective-permute-start(bf16[1,10,1,1,128]{4,3,1,2,0:T(2,128)(2,1)S(1)} %get-tuple-element.62), channel_id=1, source_target_pairs={{0,16},{16,0},{1,17},{17,1},{2,18},{18,2},{3,19},{19,3},{4,20},{20... | collective-permute-start | bytes 7688 | tf_op jit(solution)/shard_map/ppermute | solution.py:20
  42.4 0.5 collective-permute-start.7
  42.9 1.5 %collective-permute-start.5 = (f32[1,10,1,64,128]{4,3,1,2,0:T(8,128)S(1)}, f32[1,10,1,64,128]{4,3,1,2,0:T(8,128)S(1)}, u32[]{:S(2)}, u32[]{:S(2)}) collective-permute-start(f32[1,10,1,64,128]{4,3,1,2,0:T(8,128)S(1)} %get-tuple-element.21), channel_id=1, source_target_pairs={{0,1},{1,2},{2,3},{3,4},{4,5},{5,6},{6,7},{7,8},{8,9},{9,10},{10,1... | collective-permute-start | bytes 983048 | tf_op jit(solution)/shard_map/ppermute | solution.py:20
  44.5 1.3 %collective-permute-start.4 = (f32[1,10,1,64,128]{4,3,1,2,0:T(8,128)S(1)}, f32[1,10,1,64,128]{4,3,1,2,0:T(8,128)S(1)}, u32[]{:S(2)}, u32[]{:S(2)}) collective-permute-start(f32[1,10,1,64,128]{4,3,1,2,0:T(8,128)S(1)} %get-tuple-element.21), channel_id=1, source_target_pairs={{1,0},{2,1},{3,2},{4,3},{5,4},{6,5},{7,6},{8,7},{9,8},{10,9},{11,1... | collective-permute-start | bytes 983048 | tf_op jit(solution)/shard_map/ppermute | solution.py:21
  45.8 0.0 collective-permute-done.6
  45.8 0.2 collective-permute-done.7
  46.1 0.0 collective-permute-done.5
  46.1 2.3 %collective-permute-done.4 = f32[1,10,1,64,128]{4,3,1,2,0:T(8,128)S(1)} collective-permute-done((f32[1,10,1,64,128]{4,3,1,2,0:T(8,128)S(1)}, f32[1,10,1,64,128]{4,3,1,2,0:T(8,128)S(1)}, u32[]{:S(2)}, u32[]{:S(2)}) %collective-permute-start.4) | collective-permute-done | bytes 327712 | tf_op jit(solution)/shard_map/ppermute | solution.py:21
  48.5 0.0 copy-start.6
  48.5 0.1 fusion.33
  48.6 0.1 fusion.37
  48.7 0.4 fusion.17
  49.1 0.0 copy-start.2
  49.1 0.1 slice_reduce_fusion.1
  49.2 0.0 copy-done.6
  49.3 0.1 copy.84
  49.4 2.2 %scatter_custom_fusion = f32[6,4096]{0,1:T(8,128)} fusion(s32[64]{0:T(128)S(1)} %fusion.49, f32[]{:T(128)} %constant.11.clone.1, f32[6,1,64]{0,2,1:T(8,128)S(1)} %copy.84), kind=kCustom, calls=%fused_computation.1 | custom fusion | flops 384 | bytes 131076 | tf_op jit(solution)/shard_map/scatter-add | solution.py:122
  51.6 0.0 reduce-scatter.2.cloned.1.call-update
  51.6 0.0 copy-done.2
  51.6 68.0 %reduce-scatter.2.cloned.1.call-done = f32[6,256]{0,1:T(8,128)} async-done(((f32[6,4096]{0,1:T(8,128)}), f32[6,256]{0,1:T(8,128)}) %reduce-scatter.2.cloned.1.call-update) | async-done | bytes 6160 | tf_op jit(solution)/shard_map/reduce_scatter | solution.py:123
  119.6 1.6 %copy.82 = f32[1,6,256]{2,0,1:T(1,128)} copy(f32[1,6,256]{1,2,0:T(8,128)} %bitcast.82) | data formatting | bytes 12288
  (19 shorter events, 0.4 us)
Async XLA Ops:
  7.2 18.4 %copy-start = (f32[1,10,1,64,128]{4,3,2,1,0:T(8,128)S(1)}, f32[1,10,1,64,128]{4,3,2,1,0:T(8,128)}, u32[]{:S(2)}) copy-start(f32[1,10,1,64,128]{4,3,2,1,0:T(8,128)} %param.10) | copy-start | bytes 983044
  7.2 18.4 %copy-start.3 = (f32[1,1,64,128]{3,2,1,0:T(8,128)S(1)}, f32[1,1,64,128]{3,2,1,0:T(8,128)}, u32[]{:S(2)}) copy-start(f32[1,1,64,128]{3,2,1,0:T(8,128)} %param.14) | copy-start | bytes 98308
  7.2 18.4 %copy-start.7 = (s32[1,64]{1,0:T(1,128)S(1)}, s32[1,64]{1,0:T(1,128)}, u32[]{:S(2)}) copy-start(s32[1,64]{1,0:T(1,128)} %param.17) | copy-start | bytes 772
  7.2 18.4 %copy-start.8 = (s32[1,64,1]{1,2,0:T(1,128)S(1)}, s32[1,64,1]{1,2,0:T(1,128)}, u32[]{:S(2)}) copy-start(s32[1,64,1]{1,2,0:T(1,128)} %param.16) | copy-start | bytes 772
  7.2 18.6 %collective-permute-start.1 = (f32[1,10,1,64,128]{4,3,1,2,0:T(8,128)}, f32[1,10,1,64,128]{4,3,1,2,0:T(8,128)S(1)}, u32[]{:S(2)}, u32[]{:S(2)}) collective-permute-start(f32[1,10,1,64,128]{4,3,1,2,0:T(8,128)} %bitcast.71), channel_id=1, source_target_pairs={{0,1},{1,2},{2,3},{3,4},{4,5},{5,6},{6,7},{7,8},{8,9},{9,10},{10,1... | collective-permute-start | bytes 983048 | tf_op jit(solution)/shard_map/ppermute | solution.py:20
  9.8 16.0 %collective-permute-start = (f32[1,10,1,64,128]{4,3,1,2,0:T(8,128)}, f32[1,10,1,64,128]{4,3,1,2,0:T(8,128)S(1)}, u32[]{:S(2)}, u32[]{:S(2)}) collective-permute-start(f32[1,10,1,64,128]{4,3,1,2,0:T(8,128)} %bitcast.72), channel_id=1, source_target_pairs={{1,0},{2,1},{3,2},{4,3},{5,4},{6,5},{7,6},{8,7},{9,8},{10,9},{11,1... | collective-permute-start | bytes 983048 | tf_op jit(solution)/shard_map/ppermute | solution.py:21
  12.1 13.6 %collective-permute-start.2 = (bf16[1,10,1,1,128]{4,3,1,2,0:T(2,128)(2,1)S(1)}, bf16[1,10,1,1,128]{4,3,1,2,0:T(2,128)(2,1)S(1)}, u32[]{:S(2)}, u32[]{:S(2)}) collective-permute-start(bf16[1,10,1,1,128]{4,3,1,2,0:T(2,128)(2,1)S(1)} %get-tuple-element.64), channel_id=1, source_target_pairs={{0,16},{16,0},{1,17},{17,1},{2,18},{18,2},{3,19},{19,3},{4,20},{20... | collective-permute-start | bytes 7688 | tf_op jit(solution)/shard_map/ppermute | solution.py:20
  14.5 11.2 %collective-permute-start.3 = (bf16[1,10,1,1,128]{4,3,1,2,0:T(2,128)(2,1)S(1)}, bf16[1,10,1,1,128]{4,3,1,2,0:T(2,128)(2,1)S(1)}, u32[]{:S(2)}, u32[]{:S(2)}) collective-permute-start(bf16[1,10,1,1,128]{4,3,1,2,0:T(2,128)(2,1)S(1)} %get-tuple-element.65), channel_id=1, source_target_pairs={{16,0},{0,16},{17,1},{1,17},{18,2},{2,18},{19,3},{3,19},{20,4},{4,... | collective-permute-start | bytes 7688 | tf_op jit(solution)/shard_map/ppermute | solution.py:21
  16.6 23.2 %all-to-all-start = ((bf16[1,25,16,512]{3,1,0,2:T(8,128)(2,1)}), bf16[1,25,16,512]{3,1,0,2:T(8,128)(2,1)S(1)}, u32[]{:S(2)}, u32[]{:S(2)}) async-start(bf16[1,25,16,512]{3,1,0,2:T(8,128)(2,1)} %copy.66), calls=%async_computation | async-start | bytes 1048576 | tf_op jit(solution)/shard_map/all_to_all | solution.py:94
  25.5 94.1 %reduce-scatter.2.cloned.1.call-start = ((), (), s32[]{:S(2)}) async-start(), calls=%async_computation.2 | async-start | bytes 2228224 | tf_op jit(solution)/shard_map/reduce_scatter | solution.py:123
  25.8 14.6 %copy-start.1 = (f32[1,10,1,64,128]{4,3,2,1,0:T(8,128)S(1)}, f32[1,10,1,64,128]{4,3,2,1,0:T(8,128)}, u32[]{:S(2)}) copy-start(f32[1,10,1,64,128]{4,3,2,1,0:T(8,128)} %param.11) | copy-start | bytes 983044
  25.8 14.6 %copy-start.4 = (f32[1,1,64,128]{3,2,1,0:T(8,128)S(1)}, f32[1,1,64,128]{3,2,1,0:T(8,128)}, u32[]{:S(2)}) copy-start(f32[1,1,64,128]{3,2,1,0:T(8,128)} %param.13) | copy-start | bytes 98308
  25.9 14.6 %copy-start.5 = (f32[1,1,64,128]{3,2,1,0:T(8,128)S(1)}, f32[1,1,64,128]{3,2,1,0:T(8,128)}, u32[]{:S(2)}) copy-start(f32[1,1,64,128]{3,2,1,0:T(8,128)} %param.12) | copy-start | bytes 98308
  40.8 4.9 %collective-permute-start.6 = (bf16[1,10,1,1,128]{4,3,1,2,0:T(2,128)(2,1)S(1)}, bf16[1,10,1,1,128]{4,3,1,2,0:T(2,128)(2,1)S(1)}, u32[]{:S(2)}, u32[]{:S(2)}) collective-permute-start(bf16[1,10,1,1,128]{4,3,1,2,0:T(2,128)(2,1)S(1)} %get-tuple-element.62), channel_id=1, source_target_pairs={{0,16},{16,0},{1,17},{17,1},{2,18},{18,2},{3,19},{19,3},{4,20},{20... | collective-permute-start | bytes 7688 | tf_op jit(solution)/shard_map/ppermute | solution.py:20
  42.4 3.6 %collective-permute-start.7 = (bf16[1,10,1,1,128]{4,3,1,2,0:T(2,128)(2,1)S(1)}, bf16[1,10,1,1,128]{4,3,1,2,0:T(2,128)(2,1)S(1)}, u32[]{:S(2)}, u32[]{:S(2)}) collective-permute-start(bf16[1,10,1,1,128]{4,3,1,2,0:T(2,128)(2,1)S(1)} %get-tuple-element.63), channel_id=1, source_target_pairs={{16,0},{0,16},{17,1},{1,17},{18,2},{2,18},{19,3},{3,19},{20,4},{4,... | collective-permute-start | bytes 7688 | tf_op jit(solution)/shard_map/ppermute | solution.py:21
  42.9 3.1 %collective-permute-start.5 = (f32[1,10,1,64,128]{4,3,1,2,0:T(8,128)S(1)}, f32[1,10,1,64,128]{4,3,1,2,0:T(8,128)S(1)}, u32[]{:S(2)}, u32[]{:S(2)}) collective-permute-start(f32[1,10,1,64,128]{4,3,1,2,0:T(8,128)S(1)} %get-tuple-element.21), channel_id=1, source_target_pairs={{0,1},{1,2},{2,3},{3,4},{4,5},{5,6},{6,7},{7,8},{8,9},{9,10},{10,1... | collective-permute-start | bytes 983048 | tf_op jit(solution)/shard_map/ppermute | solution.py:20
  44.5 4.0 %collective-permute-start.4 = (f32[1,10,1,64,128]{4,3,1,2,0:T(8,128)S(1)}, f32[1,10,1,64,128]{4,3,1,2,0:T(8,128)S(1)}, u32[]{:S(2)}, u32[]{:S(2)}) collective-permute-start(f32[1,10,1,64,128]{4,3,1,2,0:T(8,128)S(1)} %get-tuple-element.21), channel_id=1, source_target_pairs={{1,0},{2,1},{3,2},{4,3},{5,4},{6,5},{7,6},{8,7},{9,8},{10,9},{11,1... | collective-permute-start | bytes 983048 | tf_op jit(solution)/shard_map/ppermute | solution.py:21
  48.5 0.7 copy-start.6
  49.1 2.5 %copy-start.2 = (f32[1,10,1,64,128]{4,3,1,2,0:T(8,128)}, f32[1,10,1,64,128]{4,3,1,2,0:T(8,128)S(1)}, u32[]{:S(2)}) copy-start(f32[1,10,1,64,128]{4,3,1,2,0:T(8,128)S(1)} %fusion.17) | copy-start | bytes 983044
Sparse Core Ops, SparseCore 0:
  51.7 67.8 reduce-scatter.1
where the time goes:
time: 128 us
  waiting for transfers between devices  84.5 us (66%)
  starting transfers between devices  20.1 us (16%)
  between operations  14.5 us (11%)
  other arithmetic  4.52 us (4%)
  local copies, waits for them, and re-layouts  4.46 us (3%)
    reduce_scatter x1, waiting for transfers between devices, body(): lax.psum_scatter(local_terms, 'brick', scatter_dimension=1, tiled=True)  68 us
    all_to_all x1, waiting for transfers between devices, body(): lax.all_to_all(jac_blocks, 'brick', split_axis=2, concat_axis=3, tiled=True)  13.9 us
    all_to_all x1, starting transfers between devices, body(): lax.all_to_all(jac_blocks, 'brick', split_axis=2, concat_axis=3, tiled=True)  8.92 us
    ppermute x4, starting transfers between devices, padded(): before = lax.ppermute(last, axis, up)  7.99 us
    unnamed x20, local copies, waits for them, and re-layouts  3.67 us
    ppermute x4, starting transfers between devices, padded(): after = lax.ppermute(initial, axis, down)  3.2 us
    ppermute x4, waiting for transfers between devices, padded(): after = lax.ppermute(initial, axis, down)  2.58 us
  transfers between devices with their start and end apart: 10, of which 4 were waited for; matrix products, arithmetic and copies ran while one was open for 3% of the time, Pallas kernels for 0%

commit v1 on v0

--- a/solution.py
+++ b/solution.py
@@ -91,7 +91,11 @@
     width_j = psi_start.shape[3]
     width_k = psi_start.shape[4]
     phase_angle = 2.0 * math.pi * ND * passes / BLADES
-    relaid = lax.all_to_all(jac_blocks, "brick", split_axis=2, concat_axis=3, tiled=True)
+    arr_next = lax.axis_size("brick")
+    step_out = jnp.split(jac_blocks, arr_next, axis=2)
+    next_value = jnp.stack(step_out)
+    near = lax.all_to_all(next_value, "brick", 0, 0)
+    relaid = jnp.concatenate(near, axis=3)
     tiles = relaid.reshape(1, 25, planes, width_j, width_k)
 
     def convect_fn(diff):

time: 128 us -> 135 us (1.055)
  local copies, waits for them, and re-layouts: 4.46 us -> 16.1 us
  waiting for transfers between devices: 84.5 us -> 79.1 us
    unnamed x20 -> x34, local copies, waits for them, and re-layouts: 3.67 us -> 10.7 us
    all_to_all x1, waiting for transfers between devices: 13.9 us -> 8.77 us  [body(): near = lax.all_to_all(next_value, 'brick', 0, 0)]
    split x0 -> x1, local copies, waits for them, and re-layouts: none -> 3.97 us  [body(): step_out = jnp.split(jac_blocks, arr_next, axis=2)]
    reduce_scatter x1, waiting for transfers between devices: 68 us -> 64.2 us  [body(): lax.psum_scatter(local_terms, 'brick', scatter_dimension=1, tiled=True)]
    ppermute x4, waiting for transfers between devices: 0.01 us -> 3.08 us  [padded(): before = lax.ppermute(last, axis, up)]
  transfers between devices with their start and end apart: 10 -> 10, of which waited for: 4 -> 6; matrix products, arithmetic and copies ran while one was open for 3% -> 10% of each run, Pallas kernels for 0% -> 0%
where the time goes in v1:
time: 135 us; the launch traced here: 134 us
  waiting for transfers between devices  79.1 us (59%)
  starting transfers between devices  21 us (16%)
  local copies, waits for them, and re-layouts  16.1 us (12%)
  between operations  14.4 us (11%)
  other arithmetic  3.54 us (3%)
    reduce_scatter x1, waiting for transfers between devices, body(): lax.psum_scatter(local_terms, 'brick', scatter_dimension=1, tiled=True)  64.2 us
    unnamed x34, local copies, waits for them, and re-layouts  10.7 us
    ppermute x4, starting transfers between devices, padded(): before = lax.ppermute(last, axis, up)  9.21 us
    all_to_all x1, waiting for transfers between devices, body(): near = lax.all_to_all(next_value, 'brick', 0, 0)  8.77 us
    all_to_all x1, starting transfers between devices, body(): near = lax.all_to_all(next_value, 'brick', 0, 0)  7.96 us
    split x1, local copies, waits for them, and re-layouts, body(): step_out = jnp.split(jac_blocks, arr_next, axis=2)  3.97 us
    ppermute x4, starting transfers between devices, padded(): after = lax.ppermute(initial, axis, down)  3.79 us
    ppermute x4, waiting for transfers between devices, padded(): before = lax.ppermute(last, axis, up)  3.08 us
  transfers between devices with their start and end apart: 10, of which 6 were waited for; matrix products, arithmetic and copies ran while one was open for 10% of the time, Pallas kernels for 0%

profile of v1, /device:TPU:0, one launch (start us, length us, event | category | flops | bytes accessed | tf_op | source)
XLA Modules:
  0.0 134.2 jit_solution(520305879179206095)
XLA Ops:
  7.2 0.0 copy-start
  7.2 0.0 copy-start.3
  7.2 1.4 %collective-permute-start = (f32[1,10,1,64,128]{4,3,1,2,0:T(8,128)}, f32[1,10,1,64,128]{4,3,1,2,0:T(8,128)S(1)}, u32[]{:S(2)}, u32[]{:S(2)}) collective-permute-start(f32[1,10,1,64,128]{4,3,1,2,0:T(8,128)} %bitcast.138), channel_id=1, source_target_pairs={{1,0},{2,1},{3,2},{4,3},{5,4},{6,5},{7,6},{8,7},{9,8},{10,9},{11,1... | collective-permute-start | bytes 983048 | tf_op jit(solution)/shard_map/ppermute | solution.py:21
  8.6 3.0 %collective-permute-start.1 = (f32[1,10,1,64,128]{4,3,1,2,0:T(8,128)}, f32[1,10,1,64,128]{4,3,1,2,0:T(8,128)S(1)}, u32[]{:S(2)}, u32[]{:S(2)}) collective-permute-start(f32[1,10,1,64,128]{4,3,1,2,0:T(8,128)} %bitcast.139), channel_id=1, source_target_pairs={{0,1},{1,2},{2,3},{3,4},{4,5},{5,6},{6,7},{7,8},{8,9},{9,10},{10,1... | collective-permute-start | bytes 983048 | tf_op jit(solution)/shard_map/ppermute | solution.py:20
  11.7 4.0 %fusion.52 = (bf16[1,25,1,512]{3,2,1,0:T(2,128)(2,1)S(1)}, bf16[1,25,1,512]{3,2,1,0:T(2,128)(2,1)S(1)}, bf16[1,25,1,512]{3,2,1,0:T(2,128)(2,1)S(1)}, bf16[1,25,1...) fusion(bf16[1,25,16,512]{3,2,1,0:T(8,128)(2,1)} %param.9), kind=kLoop, calls=%fused_computation.181 | loop fusion | bytes 819200 | tf_op jit(solution)/shard_map/split | solution.py:95
  15.7 0.0 copy-start.7
  15.7 0.0 copy-start.8
  15.7 0.6 constant_dynamic-update-slice_fusion.15
  16.3 0.6 constant_dynamic-update-slice_fusion.14
  16.9 0.6 constant_dynamic-update-slice_fusion.13
  17.5 0.6 constant_dynamic-update-slice_fusion.12
  18.1 0.6 constant_dynamic-update-slice_fusion.11
  18.7 0.6 constant_dynamic-update-slice_fusion.10
  19.3 0.6 constant_dynamic-update-slice_fusion.9
  19.9 0.6 constant_dynamic-update-slice_fusion.8
  20.5 0.6 constant_dynamic-update-slice_fusion.7
  21.2 0.6 constant_dynamic-update-slice_fusion.6
  21.8 0.6 constant_dynamic-update-slice_fusion.5
  22.4 0.6 constant_dynamic-update-slice_fusion.4
  23.0 0.6 constant_dynamic-update-slice_fusion.3
  23.6 0.6 constant_dynamic-update-slice_fusion.2
  24.2 0.6 constant_dynamic-update-slice_fusion.1
  24.8 0.6 constant_dynamic-update-slice_fusion
  25.4 8.0 %all-to-all-start = ((bf16[16,1,25,1,512]{4,2,3,1,0:T(8,128)(2,1)}), bf16[16,1,25,1,512]{4,2,3,1,0:T(8,128)(2,1)S(1)}, u32[]{:S(2)}, u32[]{:S(2)}) async-start(bf16[16,1,25,1,512]{4,2,3,1,0:T(8,128)(2,1)} %constant_dynamic-update-slice_fusion), calls=%async_computation | async-start | bytes 1048576 | tf_op jit(solution)/shard_map/all_to_all | solution.py:97
  33.4 0.0 reduce-scatter.2.cloned.1.call-start
  33.4 0.0 copy-done
  33.5 1.6 %collective-permute-start.2 = (bf16[1,10,1,1,128]{4,3,1,2,0:T(2,128)(2,1)S(1)}, bf16[1,10,1,1,128]{4,3,1,2,0:T(2,128)(2,1)S(1)}, u32[]{:S(2)}, u32[]{:S(2)}) collective-permute-start(bf16[1,10,1,1,128]{4,3,1,2,0:T(2,128)(2,1)S(1)} %get-tuple-element.78), channel_id=1, source_target_pairs={{0,16},{16,0},{1,17},{17,1},{2,18},{18,2},{3,19},{19,3},{4,20},{20... | collective-permute-start | bytes 7688 | tf_op jit(solution)/shard_map/ppermute | solution.py:20
  35.0 0.5 collective-permute-start.3
  35.6 0.0 copy-done.3
  35.6 0.0 copy-done.7
  35.6 0.0 copy-done.8
  35.7 1.5 %collective-permute-done.2 = bf16[1,10,1,1,128]{4,3,1,2,0:T(2,128)(2,1)S(1)} collective-permute-done((bf16[1,10,1,1,128]{4,3,1,2,0:T(2,128)(2,1)S(1)}, bf16[1,10,1,1,128]{4,3,1,2,0:T(2,128)(2,1)S(1)}, u32[]{:S(2)}, u32[]{:S(2)}) %collective-permute-start.2) | collective-permute-done | bytes 2592 | tf_op jit(solution)/shard_map/ppermute | solution.py:20
  37.2 1.5 %collective-permute-done.3 = bf16[1,10,1,1,128]{4,3,1,2,0:T(2,128)(2,1)S(1)} collective-permute-done((bf16[1,10,1,1,128]{4,3,1,2,0:T(2,128)(2,1)S(1)}, bf16[1,10,1,1,128]{4,3,1,2,0:T(2,128)(2,1)S(1)}, u32[]{:S(2)}, u32[]{:S(2)}) %collective-permute-start.3) | collective-permute-done | bytes 2592 | tf_op jit(solution)/shard_map/ppermute | solution.py:21
  38.7 0.0 collective-permute-done
  38.8 0.0 collective-permute-done.1
  38.8 0.0 copy-start.1
  38.8 0.0 copy-start.4
  38.8 0.0 copy-start.5
  38.9 8.8 %all-to-all-done = bf16[16,1,25,1,512]{4,2,3,1,0:T(8,128)(2,1)S(1)} async-done(((bf16[16,1,25,1,512]{4,2,3,1,0:T(8,128)(2,1)}), bf16[16,1,25,1,512]{4,2,3,1,0:T(8,128)(2,1)S(1)}, u32[]{:S(2)}, u32[]{:S(2)}) %all-to-all-start) | async-done | bytes 409632 | tf_op jit(solution)/shard_map/all_to_all | solution.py:97
  47.6 0.2 copy.116
  47.9 0.2 reshape_reshape.3
  48.1 0.1 fusion.25
  48.2 0.1 fusion.29
  48.3 0.0 copy-done.1
  48.4 0.3 fusion.50
  48.7 1.3 collective-permute-start.4
  50.0 3.1 %collective-permute-start.5 = (f32[1,10,1,64,128]{4,3,1,2,0:T(8,128)S(1)}, f32[1,10,1,64,128]{4,3,1,2,0:T(8,128)S(1)}, u32[]{:S(2)}, u32[]{:S(2)}) collective-permute-start(f32[1,10,1,64,128]{4,3,1,2,0:T(8,128)S(1)} %get-tuple-element.19), channel_id=1, source_target_pairs={{0,1},{1,2},{2,3},{3,4},{4,5},{5,6},{6,7},{7,8},{8,9},{9,10},{10,1... | collective-permute-start | bytes 983048 | tf_op jit(solution)/shard_map/ppermute | solution.py:20
  53.1 1.6 %collective-permute-start.6 = (bf16[1,10,1,1,128]{4,3,1,2,0:T(2,128)(2,1)S(1)}, bf16[1,10,1,1,128]{4,3,1,2,0:T(2,128)(2,1)S(1)}, u32[]{:S(2)}, u32[]{:S(2)}) collective-permute-start(bf16[1,10,1,1,128]{4,3,1,2,0:T(2,128)(2,1)S(1)} %get-tuple-element.76), channel_id=1, source_target_pairs={{0,16},{16,0},{1,17},{17,1},{2,18},{18,2},{3,19},{19,3},{4,20},{20... | collective-permute-start | bytes 7688 | tf_op jit(solution)/shard_map/ppermute | solution.py:20
  54.6 0.5 collective-permute-start.7
  55.2 1.6 %collective-permute-done.6 = bf16[1,10,1,1,128]{4,3,1,2,0:T(2,128)(2,1)S(1)} collective-permute-done((bf16[1,10,1,1,128]{4,3,1,2,0:T(2,128)(2,1)S(1)}, bf16[1,10,1,1,128]{4,3,1,2,0:T(2,128)(2,1)S(1)}, u32[]{:S(2)}, u32[]{:S(2)}) %collective-permute-start.6) | collective-permute-done | bytes 2592 | tf_op jit(solution)/shard_map/ppermute | solution.py:20
  56.7 1.5 %collective-permute-done.7 = bf16[1,10,1,1,128]{4,3,1,2,0:T(2,128)(2,1)S(1)} collective-permute-done((bf16[1,10,1,1,128]{4,3,1,2,0:T(2,128)(2,1)S(1)}, bf16[1,10,1,1,128]{4,3,1,2,0:T(2,128)(2,1)S(1)}, u32[]{:S(2)}, u32[]{:S(2)}) %collective-permute-start.7) | collective-permute-done | bytes 2592 | tf_op jit(solution)/shard_map/ppermute | solution.py:21
  58.3 0.0 collective-permute-done.4
  58.3 0.0 collective-permute-done.5
  58.4 0.0 copy-start.6
  58.4 0.1 fusion.33
  58.5 0.1 fusion.37
  58.6 0.4 fusion.17
  59.0 0.0 copy-start.2
  59.0 0.1 slice_reduce_fusion.1
  59.2 0.1 copy.149
  59.3 2.2 %scatter_custom_fusion = f32[6,4096]{0,1:T(8,128)} fusion(s32[64]{0:T(128)S(1)} %fusion.49, f32[]{:T(128)} %constant.11.clone.1, f32[6,1,64]{0,2,1:T(8,128)S(1)} %copy.149), kind=kCustom, calls=%fused_computation.1 | custom fusion | flops 384 | bytes 131076 | tf_op jit(solution)/shard_map/scatter-add | solution.py:126
  61.5 0.0 reduce-scatter.2.cloned.1.call-update
  61.5 64.2 %reduce-scatter.2.cloned.1.call-done = f32[6,256]{0,1:T(8,128)} async-done(((f32[6,4096]{0,1:T(8,128)}), f32[6,256]{0,1:T(8,128)}) %reduce-scatter.2.cloned.1.call-update) | async-done | bytes 6160 | tf_op jit(solution)/shard_map/reduce_scatter | solution.py:127
  125.7 1.6 %copy.131 = f32[1,6,256]{2,0,1:T(1,128)} copy(f32[1,6,256]{1,2,0:T(8,128)} %bitcast.150) | data formatting | bytes 12288
  (24 shorter events, 0.4 us)
Async XLA Ops:
  7.2 26.3 %copy-start = (f32[1,10,1,64,128]{4,3,2,1,0:T(8,128)S(1)}, f32[1,10,1,64,128]{4,3,2,1,0:T(8,128)}, u32[]{:S(2)}) copy-start(f32[1,10,1,64,128]{4,3,2,1,0:T(8,128)} %param.10) | copy-start | bytes 983044
  7.2 28.4 %copy-start.3 = (f32[1,1,64,128]{3,2,1,0:T(8,128)S(1)}, f32[1,1,64,128]{3,2,1,0:T(8,128)}, u32[]{:S(2)}) copy-start(f32[1,1,64,128]{3,2,1,0:T(8,128)} %param.14) | copy-start | bytes 98308
  7.2 31.6 %collective-permute-start = (f32[1,10,1,64,128]{4,3,1,2,0:T(8,128)}, f32[1,10,1,64,128]{4,3,1,2,0:T(8,128)S(1)}, u32[]{:S(2)}, u32[]{:S(2)}) collective-permute-start(f32[1,10,1,64,128]{4,3,1,2,0:T(8,128)} %bitcast.138), channel_id=1, source_target_pairs={{1,0},{2,1},{3,2},{4,3},{5,4},{6,5},{7,6},{8,7},{9,8},{10,9},{11,1... | collective-permute-start | bytes 983048 | tf_op jit(solution)/shard_map/ppermute | solution.py:21
  8.6 30.1 %collective-permute-start.1 = (f32[1,10,1,64,128]{4,3,1,2,0:T(8,128)}, f32[1,10,1,64,128]{4,3,1,2,0:T(8,128)S(1)}, u32[]{:S(2)}, u32[]{:S(2)}) collective-permute-start(f32[1,10,1,64,128]{4,3,1,2,0:T(8,128)} %bitcast.139), channel_id=1, source_target_pairs={{0,1},{1,2},{2,3},{3,4},{4,5},{5,6},{6,7},{7,8},{8,9},{9,10},{10,1... | collective-permute-start | bytes 983048 | tf_op jit(solution)/shard_map/ppermute | solution.py:20
  15.7 20.0 %copy-start.7 = (s32[1,64]{1,0:T(1,128)S(1)}, s32[1,64]{1,0:T(1,128)}, u32[]{:S(2)}) copy-start(s32[1,64]{1,0:T(1,128)} %param.17) | copy-start | bytes 772
  15.7 20.0 %copy-start.8 = (s32[1,64,1]{1,2,0:T(1,128)S(1)}, s32[1,64,1]{1,2,0:T(1,128)}, u32[]{:S(2)}) copy-start(s32[1,64,1]{1,2,0:T(1,128)} %param.16) | copy-start | bytes 772
  25.4 22.2 %all-to-all-start = ((bf16[16,1,25,1,512]{4,2,3,1,0:T(8,128)(2,1)}), bf16[16,1,25,1,512]{4,2,3,1,0:T(8,128)(2,1)S(1)}, u32[]{:S(2)}, u32[]{:S(2)}) async-start(bf16[16,1,25,1,512]{4,2,3,1,0:T(8,128)(2,1)} %constant_dynamic-update-slice_fusion), calls=%async_computation | async-start | bytes 1048576 | tf_op jit(solution)/shard_map/all_to_all | solution.py:97
  33.4 92.4 %reduce-scatter.2.cloned.1.call-start = ((), (), s32[]{:S(2)}) async-start(), calls=%async_computation.2 | async-start | bytes 2228224 | tf_op jit(solution)/shard_map/reduce_scatter | solution.py:127
  33.5 3.7 %collective-permute-start.2 = (bf16[1,10,1,1,128]{4,3,1,2,0:T(2,128)(2,1)S(1)}, bf16[1,10,1,1,128]{4,3,1,2,0:T(2,128)(2,1)S(1)}, u32[]{:S(2)}, u32[]{:S(2)}) collective-permute-start(bf16[1,10,1,1,128]{4,3,1,2,0:T(2,128)(2,1)S(1)} %get-tuple-element.78), channel_id=1, source_target_pairs={{0,16},{16,0},{1,17},{17,1},{2,18},{18,2},{3,19},{19,3},{4,20},{20... | collective-permute-start | bytes 7688 | tf_op jit(solution)/shard_map/ppermute | solution.py:20
  35.0 3.6 %collective-permute-start.3 = (bf16[1,10,1,1,128]{4,3,1,2,0:T(2,128)(2,1)S(1)}, bf16[1,10,1,1,128]{4,3,1,2,0:T(2,128)(2,1)S(1)}, u32[]{:S(2)}, u32[]{:S(2)}) collective-permute-start(bf16[1,10,1,1,128]{4,3,1,2,0:T(2,128)(2,1)S(1)} %get-tuple-element.79), channel_id=1, source_target_pairs={{16,0},{0,16},{17,1},{1,17},{18,2},{2,18},{19,3},{3,19},{20,4},{4,... | collective-permute-start | bytes 7688 | tf_op jit(solution)/shard_map/ppermute | solution.py:21
  38.8 9.5 %copy-start.1 = (f32[1,10,1,64,128]{4,3,2,1,0:T(8,128)S(1)}, f32[1,10,1,64,128]{4,3,2,1,0:T(8,128)}, u32[]{:S(2)}) copy-start(f32[1,10,1,64,128]{4,3,2,1,0:T(8,128)} %param.11) | copy-start | bytes 983044
  38.8 9.5 %copy-start.4 = (f32[1,1,64,128]{3,2,1,0:T(8,128)S(1)}, f32[1,1,64,128]{3,2,1,0:T(8,128)}, u32[]{:S(2)}) copy-start(f32[1,1,64,128]{3,2,1,0:T(8,128)} %param.13) | copy-start | bytes 98308
  38.8 9.5 %copy-start.5 = (f32[1,1,64,128]{3,2,1,0:T(8,128)S(1)}, f32[1,1,64,128]{3,2,1,0:T(8,128)}, u32[]{:S(2)}) copy-start(f32[1,1,64,128]{3,2,1,0:T(8,128)} %param.12) | copy-start | bytes 98308
  48.7 9.6 %collective-permute-start.4 = (f32[1,10,1,64,128]{4,3,1,2,0:T(8,128)S(1)}, f32[1,10,1,64,128]{4,3,1,2,0:T(8,128)S(1)}, u32[]{:S(2)}, u32[]{:S(2)}) collective-permute-start(f32[1,10,1,64,128]{4,3,1,2,0:T(8,128)S(1)} %get-tuple-element.19), channel_id=1, source_target_pairs={{1,0},{2,1},{3,2},{4,3},{5,4},{6,5},{7,6},{8,7},{9,8},{10,9},{11,1... | collective-permute-start | bytes 983048 | tf_op jit(solution)/shard_map/ppermute | solution.py:21
  50.0 8.4 %collective-permute-start.5 = (f32[1,10,1,64,128]{4,3,1,2,0:T(8,128)S(1)}, f32[1,10,1,64,128]{4,3,1,2,0:T(8,128)S(1)}, u32[]{:S(2)}, u32[]{:S(2)}) collective-permute-start(f32[1,10,1,64,128]{4,3,1,2,0:T(8,128)S(1)} %get-tuple-element.19), channel_id=1, source_target_pairs={{0,1},{1,2},{2,3},{3,4},{4,5},{5,6},{6,7},{7,8},{8,9},{9,10},{10,1... | collective-permute-start | bytes 983048 | tf_op jit(solution)/shard_map/ppermute | solution.py:20
  53.1 3.7 %collective-permute-start.6 = (bf16[1,10,1,1,128]{4,3,1,2,0:T(2,128)(2,1)S(1)}, bf16[1,10,1,1,128]{4,3,1,2,0:T(2,128)(2,1)S(1)}, u32[]{:S(2)}, u32[]{:S(2)}) collective-permute-start(bf16[1,10,1,1,128]{4,3,1,2,0:T(2,128)(2,1)S(1)} %get-tuple-element.76), channel_id=1, source_target_pairs={{0,16},{16,0},{1,17},{17,1},{2,18},{18,2},{3,19},{19,3},{4,20},{20... | collective-permute-start | bytes 7688 | tf_op jit(solution)/shard_map/ppermute | solution.py:20
  54.6 3.6 %collective-permute-start.7 = (bf16[1,10,1,1,128]{4,3,1,2,0:T(2,128)(2,1)S(1)}, bf16[1,10,1,1,128]{4,3,1,2,0:T(2,128)(2,1)S(1)}, u32[]{:S(2)}, u32[]{:S(2)}) collective-permute-start(bf16[1,10,1,1,128]{4,3,1,2,0:T(2,128)(2,1)S(1)} %get-tuple-element.77), channel_id=1, source_target_pairs={{16,0},{0,16},{17,1},{1,17},{18,2},{2,18},{19,3},{3,19},{20,4},{4,... | collective-permute-start | bytes 7688 | tf_op jit(solution)/shard_map/ppermute | solution.py:21
  58.4 0.7 copy-start.6
  59.0 2.5 %copy-start.2 = (f32[1,10,1,64,128]{4,3,1,2,0:T(8,128)}, f32[1,10,1,64,128]{4,3,1,2,0:T(8,128)S(1)}, u32[]{:S(2)}) copy-start(f32[1,10,1,64,128]{4,3,1,2,0:T(8,128)S(1)} %fusion.17) | copy-start | bytes 983044
Sparse Core Ops, SparseCore 0:
  61.6 64.0 reduce-scatter.1
